TPU v7x, 32 devices: a whole 2x2x4 slice. The times are simulated.
32 devices in a mesh: orb: 4 (over y, x), grid: 8 (over z, core).
Axes of the slice: x: 2, y: 2, z: 4, core: 2. Of those that a mesh axis runs over, the one named last changes fastest.
Arguments:
- orbitals: float32 [4, 96, 192, 256], P('orb', 'grid'), may hold values from -6 to 6
- potential: float32 [96, 192, 256], P('grid'), may hold values from -4 to 0
- trial_potential: float32 [96, 192, 256], P('grid'), may hold values from -6 to 6
- eigenvalues: float32 [4], P('orb'), may hold values from -3 to 0
- frequency: float32 [1], replicated, may hold values from 1 to 8
Outputs:
- solutions: float32 [4, 96, 192, 256], P('orb', 'grid')
- density: float32 [96, 192, 256], P('grid', 'orb')
All inputs are finite; a program needn't handle non-finite values.
Results may differ from a plain program's by a relative error of at most 0.0001.
Values sent between devices are 32-bit elements; how exact they have to be, the bound alone decides.
A program may use at most 192 MiB of HBM per device.

v0:
```python
import jax
import jax.numpy as jnp
from jax import lax
from jax.sharding import PartitionSpec as P

ITERS = 2


STENCIL = (
    -5369.0 / 1800.0,
    12.0 / 7.0,
    -15.0 / 56.0,
    10.0 / 189.0,
    -1.0 / 112.0,
    2.0 / 1925.0,
    -1.0 / 16632.0,
)
SPACING = 0.75


def extended(value, sides, width):
    for axis, dim in sides:
        count, length = (lax.axis_size(axis), value.shape[dim])
        up = [(i, (i + 1) % count) for i in range(count - 1)]
        down = [(j, i) for i, j in up]
        last = lax.slice_in_dim(value, length - width, length, axis=dim)
        leading = lax.slice_in_dim(value, 0, width, axis=dim)
        before = lax.ppermute(last, axis, up)
        after = lax.ppermute(leading, axis, down)
        value = jnp.concatenate([before, value, after], axis=dim)
    return value


def shifted_hamiltonian(padded, potential, energy):
    axis_rows = padded.ndim - 3
    axis_cols = padded.ndim - 2
    length = padded.shape[axis_rows] - 12
    width = padded.shape[axis_cols]
    wrapped = jnp.concatenate(
        [padded[..., width - 6 :, :], padded, padded[..., :6, :]], axis=axis_cols
    )

    def take(row_off, col_off):
        part = lax.slice_in_dim(wrapped, 6 + row_off, 6 + row_off + length, axis=axis_rows)
        return lax.slice_in_dim(part, 6 + col_off, 6 + col_off + width, axis=axis_cols)

    center = take(0, 0)
    summed = 3.0 * STENCIL[0] * center
    for offset in range(1, 7):
        beside_all = take(offset, 0) + take(-offset, 0) + take(0, offset) + take(0, -offset)
        beside_all = beside_all + jnp.roll(center, offset, -1) + jnp.roll(center, -offset, -1)
        summed = summed + STENCIL[offset] * beside_all
    return -0.5 / (SPACING * SPACING) * summed + (potential - energy) * center


def cell_sum(first, second):
    return jnp.sum(first * second, axis=(1, 2, 3))


def spread(values):
    return values[:, None, None, None]


def body(orbitals, potential, trial_potential, eigenvalues, frequency):
    squared = frequency[0] * frequency[0]
    energy = spread(eigenvalues)

    def shifted(field):
        padded = extended(field, (("grid", 1),), 6)
        return shifted_hamiltonian(padded, potential, energy)

    def operator(field):
        return shifted(shifted(field)) + squared * field

    source = trial_potential * orbitals
    solution = jnp.zeros_like(source)
    residual = source

    def paired(vector, image):
        return lax.psum((cell_sum(vector, vector), cell_sum(vector, image)), "grid")

    image = operator(residual)
    norm_now, product = paired(residual, image)
    step_size = norm_now / product
    direction = residual
    along = image
    for step in range(ITERS):
        solution = solution + spread(step_size) * direction
        residual = residual - spread(step_size) * along
        if step + 1 < ITERS:
            image = operator(residual)
            norm_next, product = paired(residual, image)
            ratio = norm_next / norm_now
            step_size = norm_next / (product - ratio * norm_next / step_size)
            direction = residual + spread(ratio) * direction
            along = image + spread(ratio) * along
            norm_now = norm_next
    response = -4.0 * jnp.sum(orbitals * shifted(solution), axis=0)
    density = lax.psum_scatter(response, "orb", scatter_dimension=1, tiled=True)
    return (solution, density)


def solution(mesh):
    in_specs = (
        P("orb", "grid", None, None),
        P("grid", None, None),
        P("grid", None, None),
        P("orb"),
        P(),
    )
    out_specs = (P("orb", "grid", None, None), P("grid", "orb", None))
    return jax.shard_map(body, mesh=mesh, in_specs=in_specs, out_specs=out_specs, check_vma=False)
```

profile of v0, /device:TPU:0, one launch (start us, length us, event | category | flops | bytes accessed | tf_op | source)
XLA Modules:
  0.0 439.2 jit_solution(17979455613809913203)
XLA Ops:
  7.2 2.7 bitcast_multiply_fusion.5
  11.4 3.1 collective-permute-start.1
  21.6 1.8 fusion.333
  25.2 3.0 fusion.336
  28.2 2.9 fusion.330
  31.1 3.0 fusion.338
  35.5 3.0 fusion.334
  38.4 3.0 fusion.340
  41.4 3.0 fusion.332
  44.5 3.3 fusion.9
  47.8 23.1 %fusion.218 = f32[1,12,192,256]{3,2,1,0:T(8,128)S(1)} fusion(f32[1,12,192,256]{3,2,1,0:T(8,128)S(1)} %bitcast_multiply_fusion.5, f32[1,6,192,256]{3,2,1,0:T(8,128)} %copy-done.4, f32[1,6,192,256]{3,2,1,0:T(8,128)S(1)} %collective-permute-done, f32[1,24,198,256]{3,2,1,0:T(8,128)} %get-tuple-element.20, f32[1,24,198,256]{3,2,1,0:T(8,128)S(1)} %get-tuple-element.19, ...), kind=kLoop, calls=%fused_computation.338 | loop fusion | flops 41877504 | bytes 66060292 | tf_op jit(solution)/shard_map/add | solution.py:53
  74.5 1.9 fusion.319
  80.0 1.8 fusion.328
  82.0 2.9 fusion.324
  84.9 3.0 fusion.320
  87.9 3.0 fusion.326
  90.9 4.6 %collective-permute-start.3 = (f32[1,6,192,256]{3,2,1,0:T(8,128)S(1)}, f32[1,6,192,256]{3,2,1,0:T(8,128)S(1)}, u32[]{:S(2)}, u32[]{:S(2)}) collective-permute-start(f32[1,6,192,256]{3,2,1,0:T(8,128)S(1)} %get-tuple-element.119), channel_id=1, source_target_pairs={{0,1},{1,2},{2,3},{3,4},{4,5},{5,6},{6,7},{8,9},{9,10},{10,11},{11... | collective-permute-start | bytes 3538952 | tf_op jit(solution)/shard_map/ppermute | solution.py:28
  96.7 3.0 fusion.318
  99.7 2.9 fusion.322
  102.6 3.0 fusion.329
  105.6 3.1 fusion.7
  108.7 24.7 %multiply_reduce_fusion.1 = (f32[]{:T(128)}, f32[]{:T(128)}, f32[1,12,192,256]{3,2,1,0:T(8,128)}) fusion(f32[1,12,192,256]{3,2,1,0:T(8,128)S(1)} %bitcast_multiply_fusion.5, f32[]{:T(128)} %bitcast.4, f32[1,12,192,256]{3,2,1,0:T(8,128)S(1)} %fusion.218, f32[12,192,256]{2,1,0:T(8,128)} %param.6, f32[]{:T(128)} %bitcast.36, ...), kind=kLoop, calls=%fused_computation.425 | loop fusion | flops 45416448 | bytes 68419600 | tf_op jit(solution)/shard_map/reduce_sum | solution.py:57
  133.4 22.0 %all-reduce.1 = (f32[1]{0:T(128)}, f32[1]{0:T(128)}) all-reduce(f32[1]{0:T(128)} %bitcast.1, f32[1]{0:T(128)} %bitcast.5), channel_id=1, replica_groups=mesh['orb'=4,'grid'=8] {'grid'}, use_global_device_ids=true, to_apply=%region_1.2 | all-reduce | flops 2 | bytes 16 | tf_op jit(solution)/shard_map/psum | solution.py:80
  156.7 2.9 multiply_reduce_fusion
  159.6 2.1 fusion.307
  165.2 1.8 fusion.315
  167.1 1.9 fusion.311
  168.9 1.9 fusion.305
  170.9 2.9 fusion.312
  173.8 2.9 fusion.308
  176.8 2.9 fusion.306
  181.0 3.1 collective-permute-start.5
  184.1 3.0 fusion.314
  187.1 3.0 fusion.304
  190.0 2.9 fusion.310
  193.0 4.6 %fusion.5 = (f32[1,24,198,256]{3,2,1,0:T(8,128)}, f32[1,24,198,256]{3,2,1,0:T(8,128)}) fusion(f32[1,6,192,256]{3,2,1,0:T(8,128)S(1)} %collective-permute-done.4, f32[1,12,192,256]{3,2,1,0:T(8,128)S(1)} %get-tuple-element.9, f32[1,6,192,256]{3,2,1,0:T(8,128)S(1)} %collective-permute-done.5), kind=kLoop, calls=%fused_computation.116 | loop fusion | flops 12165120 | bytes 14450688 | tf_op jit(solution)/shard_map/concatenate | solution.py:39
  197.6 28.6 %fusion.121 = f32[1,12,192,256]{3,2,1,0:T(8,128)S(1)} fusion(f32[1,12,192,256]{3,2,1,0:T(8,128)S(1)} %get-tuple-element.9, f32[1,6,192,256]{3,2,1,0:T(8,128)} %copy-done.8, f32[1,6,192,256]{3,2,1,0:T(8,128)S(1)} %collective-permute-done.4, f32[1,24,198,256]{3,2,1,0:T(8,128)} %get-tuple-element.16, f32[1,24,198,256]{3,2,1,0:T(8,128)} %get-tuple-element.15, ...), kind=kLoop, calls=%fused_computation.241 | loop fusion | flops 41877504 | bytes 66060292 | tf_op jit(solution)/shard_map/add | solution.py:53
  228.0 1.9 fusion.297
  231.6 1.8 fusion.299
  233.5 1.8 fusion.291
  237.3 3.0 fusion.298
  240.3 2.9 fusion.294
  243.3 2.9 fusion.300
  246.1 6.1 %collective-permute-start.7 = (f32[1,6,192,256]{3,2,1,0:T(8,128)S(1)}, f32[1,6,192,256]{3,2,1,0:T(8,128)S(1)}, u32[]{:S(2)}, u32[]{:S(2)}) collective-permute-start(f32[1,6,192,256]{3,2,1,0:T(8,128)S(1)} %get-tuple-element.67), channel_id=1, source_target_pairs={{0,1},{1,2},{2,3},{3,4},{4,5},{5,6},{6,7},{8,9},{9,10},{10,11},{11... | collective-permute-start | bytes 3538952 | tf_op jit(solution)/shard_map/ppermute | solution.py:28
  253.6 2.9 fusion.292
  256.5 3.0 fusion.296
  259.5 3.0 fusion.303
  262.5 4.7 %fusion.3 = (f32[1,24,198,256]{3,2,1,0:T(8,128)}, f32[1,24,198,256]{3,2,1,0:T(8,128)}) fusion(f32[1,6,192,256]{3,2,1,0:T(8,128)S(1)} %collective-permute-done.6, f32[1,12,192,256]{3,2,1,0:T(8,128)S(1)} %fusion.121, f32[1,6,192,256]{3,2,1,0:T(8,128)S(1)} %collective-permute-done.7), kind=kLoop, calls=%fused_computation.110 | loop fusion | flops 12165120 | bytes 14450688 | tf_op jit(solution)/shard_map/concatenate | solution.py:39
  267.1 32.0 %fusion.276 = f32[]{:T(128)} fusion(f32[1,12,192,256]{3,2,1,0:T(8,128)S(1)} %get-tuple-element.9, f32[1,12,192,256]{3,2,1,0:T(8,128)S(1)} %fusion.121, f32[1,12,192,6]{3,2,1,0:T(8,128)} %get-tuple-element.70, f32[1,12,192,250]{3,2,1,0:T(8,128)} %get-tuple-element.72, f32[1,12,192,250]{3,2,1,0:T(8,128)} %get-tuple-element.71, ...), kind=kLoop, calls=%fused_computation.427 | loop fusion | flops 44236800 | bytes 66060300 | tf_op jit(solution)/shard_map/reduce_sum | solution.py:57
  299.2 23.9 %all-reduce = (f32[1]{0:T(128)}, f32[1]{0:T(128)}) all-reduce(f32[1]{0:T(128)} %bitcast.7, f32[1]{0:T(128)} %bitcast.8), channel_id=1, replica_groups=mesh['orb'=4,'grid'=8] {'grid'}, use_global_device_ids=true, to_apply=%region_5.6 | all-reduce | flops 2 | bytes 16 | tf_op jit(solution)/shard_map/psum | solution.py:80
  327.6 2.1 multiply_add_fusion
  329.7 2.1 fusion.281
  331.7 1.9 fusion.283
  333.6 1.9 fusion.287
  341.0 3.0 fusion.286
  344.0 2.9 fusion.282
  346.9 2.9 fusion.280
  351.1 3.1 collective-permute-start.9
  354.2 3.0 fusion.288
  357.2 2.9 fusion.278
  360.1 2.9 fusion.284
  363.0 3.2 fusion.1
  366.2 23.9 %fusion.23 = f32[12,192,256]{2,1,0:T(8,128)} fusion(f32[1,12,192,256]{3,2,1,0:T(8,128)} %param.5, f32[1,12,192,256]{3,2,1,0:T(8,128)S(1)} %multiply_add_fusion, f32[1,6,192,256]{3,2,1,0:T(8,128)} %copy-done.7, f32[1,6,192,256]{3,2,1,0:T(8,128)S(1)} %collective-permute-done.8, f32[1,24,198,256]{3,2,1,0:T(8,128)} %get-tuple-element.12, ...), kind=kLoop, calls=%fused_computation.143 | loop fusion | flops 43057152 | bytes 68419584 | tf_op jit(solution)/shard_map/mul | solution.py:98
  390.1 41.8 %reduce-scatter.2.cloned.1.call-done = f32[12,48,256]{2,1,0:T(8,128)} async-done(((f32[12,192,256]{2,1,0:T(8,128)}), f32[12,48,256]{2,1,0:T(8,128)}) %reduce-scatter.2.cloned.1.call-update) | async-done | bytes 589840 | tf_op jit(solution)/shard_map/reduce_scatter | solution.py:99
  (57 shorter events, 37.9 us)
Async XLA Ops:
  7.2 424.7 %reduce-scatter.2.cloned.1.call-start = ((), (), s32[]{:S(2)}) async-start(), calls=%async_computation.1 | async-start | bytes 2949120 | tf_op jit(solution)/shard_map/reduce_scatter | solution.py:99
  10.1 34.4 %collective-permute-start = (f32[1,6,192,256]{3,2,1,0:T(8,128)S(1)}, f32[1,6,192,256]{3,2,1,0:T(8,128)S(1)}, u32[]{:S(2)}, u32[]{:S(2)}) collective-permute-start(f32[1,6,192,256]{3,2,1,0:T(8,128)S(1)} %get-tuple-element.149), channel_id=1, source_target_pairs={{1,0},{2,1},{3,2},{4,3},{5,4},{6,5},{7,6},{9,8},{10,9},{11,10},{12... | collective-permute-start | bytes 3538952 | tf_op jit(solution)/shard_map/ppermute | solution.py:29
  11.4 33.1 %collective-permute-start.1 = (f32[1,6,192,256]{3,2,1,0:T(8,128)S(1)}, f32[1,6,192,256]{3,2,1,0:T(8,128)S(1)}, u32[]{:S(2)}, u32[]{:S(2)}) collective-permute-start(f32[1,6,192,256]{3,2,1,0:T(8,128)S(1)} %get-tuple-element.150), channel_id=1, source_target_pairs={{0,1},{1,2},{2,3},{3,4},{4,5},{5,6},{6,7},{8,9},{9,10},{10,11},{11... | collective-permute-start | bytes 3538952 | tf_op jit(solution)/shard_map/ppermute | solution.py:28
  44.5 3.3 copy-start.4
  90.9 14.7 %collective-permute-start.3 = (f32[1,6,192,256]{3,2,1,0:T(8,128)S(1)}, f32[1,6,192,256]{3,2,1,0:T(8,128)S(1)}, u32[]{:S(2)}, u32[]{:S(2)}) collective-permute-start(f32[1,6,192,256]{3,2,1,0:T(8,128)S(1)} %get-tuple-element.119), channel_id=1, source_target_pairs={{0,1},{1,2},{2,3},{3,4},{4,5},{5,6},{6,7},{8,9},{9,10},{10,11},{11... | collective-permute-start | bytes 3538952 | tf_op jit(solution)/shard_map/ppermute | solution.py:28
  95.4 10.2 %collective-permute-start.2 = (f32[1,6,192,256]{3,2,1,0:T(8,128)S(1)}, f32[1,6,192,256]{3,2,1,0:T(8,128)S(1)}, u32[]{:S(2)}, u32[]{:S(2)}) collective-permute-start(f32[1,6,192,256]{3,2,1,0:T(8,128)S(1)} %get-tuple-element.120), channel_id=1, source_target_pairs={{1,0},{2,1},{3,2},{4,3},{5,4},{6,5},{7,6},{9,8},{10,9},{11,10},{12... | collective-permute-start | bytes 3538952 | tf_op jit(solution)/shard_map/ppermute | solution.py:29
  105.6 3.1 copy-start.5
  159.6 107.5 %copy-start = (f32[1,12,192,256]{3,2,1,0:T(8,128)}, f32[1,12,192,256]{3,2,1,0:T(8,128)S(1)}, u32[]{:S(2)}) copy-start(f32[1,12,192,256]{3,2,1,0:T(8,128)S(1)} %get-tuple-element.9) | copy-start | bytes 7077892
  179.7 13.3 %collective-permute-start.4 = (f32[1,6,192,256]{3,2,1,0:T(8,128)S(1)}, f32[1,6,192,256]{3,2,1,0:T(8,128)S(1)}, u32[]{:S(2)}, u32[]{:S(2)}) collective-permute-start(f32[1,6,192,256]{3,2,1,0:T(8,128)S(1)} %get-tuple-element.97), channel_id=1, source_target_pairs={{1,0},{2,1},{3,2},{4,3},{5,4},{6,5},{7,6},{9,8},{10,9},{11,10},{12... | collective-permute-start | bytes 3538952 | tf_op jit(solution)/shard_map/ppermute | solution.py:29
  181.0 12.0 %collective-permute-start.5 = (f32[1,6,192,256]{3,2,1,0:T(8,128)S(1)}, f32[1,6,192,256]{3,2,1,0:T(8,128)S(1)}, u32[]{:S(2)}, u32[]{:S(2)}) collective-permute-start(f32[1,6,192,256]{3,2,1,0:T(8,128)S(1)} %get-tuple-element.98), channel_id=1, source_target_pairs={{0,1},{1,2},{2,3},{3,4},{4,5},{5,6},{6,7},{8,9},{9,10},{10,11},{11... | collective-permute-start | bytes 3538952 | tf_op jit(solution)/shard_map/ppermute | solution.py:28
  192.9 4.6 %copy-start.2 = (f32[12,192,256]{2,1,0:T(8,128)S(1)}, f32[12,192,256]{2,1,0:T(8,128)}, u32[]{:S(2)}) copy-start(f32[12,192,256]{2,1,0:T(8,128)} %param.6) | copy-start | bytes 7077892
  193.0 4.6 %copy-start.8 = (f32[1,6,192,256]{3,2,1,0:T(8,128)}, f32[1,6,192,256]{3,2,1,0:T(8,128)S(1)}, u32[]{:S(2)}) copy-start(f32[1,6,192,256]{3,2,1,0:T(8,128)S(1)} %collective-permute-done.5) | copy-start | bytes 3538948
  246.1 16.3 %collective-permute-start.7 = (f32[1,6,192,256]{3,2,1,0:T(8,128)S(1)}, f32[1,6,192,256]{3,2,1,0:T(8,128)S(1)}, u32[]{:S(2)}, u32[]{:S(2)}) collective-permute-start(f32[1,6,192,256]{3,2,1,0:T(8,128)S(1)} %get-tuple-element.67), channel_id=1, source_target_pairs={{0,1},{1,2},{2,3},{3,4},{4,5},{5,6},{6,7},{8,9},{9,10},{10,11},{11... | collective-permute-start | bytes 3538952 | tf_op jit(solution)/shard_map/ppermute | solution.py:28
  252.3 10.2 %collective-permute-start.6 = (f32[1,6,192,256]{3,2,1,0:T(8,128)S(1)}, f32[1,6,192,256]{3,2,1,0:T(8,128)S(1)}, u32[]{:S(2)}, u32[]{:S(2)}) collective-permute-start(f32[1,6,192,256]{3,2,1,0:T(8,128)S(1)} %get-tuple-element.68), channel_id=1, source_target_pairs={{1,0},{2,1},{3,2},{4,3},{5,4},{6,5},{7,6},{9,8},{10,9},{11,10},{12... | collective-permute-start | bytes 3538952 | tf_op jit(solution)/shard_map/ppermute | solution.py:29
  262.5 4.7 %copy-start.6 = (f32[1,6,192,256]{3,2,1,0:T(8,128)}, f32[1,6,192,256]{3,2,1,0:T(8,128)S(1)}, u32[]{:S(2)}) copy-start(f32[1,6,192,256]{3,2,1,0:T(8,128)S(1)} %collective-permute-done.6) | copy-start | bytes 3538948
  329.7 36.5 %copy-start.1 = (f32[1,12,192,256]{3,2,1,0:T(8,128)}, f32[1,12,192,256]{3,2,1,0:T(8,128)S(1)}, u32[]{:S(2)}) copy-start(f32[1,12,192,256]{3,2,1,0:T(8,128)S(1)} %multiply_add_fusion) | copy-start | bytes 7077892
  349.8 13.2 %collective-permute-start.8 = (f32[1,6,192,256]{3,2,1,0:T(8,128)S(1)}, f32[1,6,192,256]{3,2,1,0:T(8,128)S(1)}, u32[]{:S(2)}, u32[]{:S(2)}) collective-permute-start(f32[1,6,192,256]{3,2,1,0:T(8,128)S(1)} %get-tuple-element.45), channel_id=1, source_target_pairs={{1,0},{2,1},{3,2},{4,3},{5,4},{6,5},{7,6},{9,8},{10,9},{11,10},{12... | collective-permute-start | bytes 3538952 | tf_op jit(solution)/shard_map/ppermute | solution.py:29
  351.1 11.9 %collective-permute-start.9 = (f32[1,6,192,256]{3,2,1,0:T(8,128)S(1)}, f32[1,6,192,256]{3,2,1,0:T(8,128)S(1)}, u32[]{:S(2)}, u32[]{:S(2)}) collective-permute-start(f32[1,6,192,256]{3,2,1,0:T(8,128)S(1)} %get-tuple-element.46), channel_id=1, source_target_pairs={{0,1},{1,2},{2,3},{3,4},{4,5},{5,6},{6,7},{8,9},{9,10},{10,11},{11... | collective-permute-start | bytes 3538952 | tf_op jit(solution)/shard_map/ppermute | solution.py:28
  363.0 3.2 copy-start.3
  363.0 3.2 copy-start.7
Sparse Core Ops, SparseCore 0:
  390.2 41.5 reduce-scatter.1
where the time goes:
time: 445 us; the launch traced here: 439 us
  other arithmetic  159 us (36%)
  local copies, waits for them, and re-layouts  144 us (32%)
  blocking collectives  45.9 us (10%)
  waiting for transfers between devices  41.8 us (9%)
  starting transfers between devices  26.5 us (6%)
  between operations  21.8 us (5%)
    slice x36, local copies, waits for them, and re-layouts, shifted_hamiltonian(): jnp.roll(center, -offset, -1)  86.2 us
    reduce_sum x3, other arithmetic, cell_sum(): return jnp.sum(first * second, axis=(1, 2, 3))  59.6 us
    slice x24, local copies, waits for them, and re-layouts, shifted_hamiltonian(): jnp.roll(center, offset, -1)  57.2 us
    add x2, other arithmetic, shifted_hamiltonian(): return -0.5 / (SPACING * SPACING) * summed + (potential - energy) * center  51.7 us
    psum x2, blocking collectives, paired(): return lax.psum((cell_sum(vector, vector), cell_sum(vector, image)), 'grid')  45.9 us
    reduce_scatter x1, waiting for transfers between devices, body(): density = lax.psum_scatter(response, 'orb', scatter_dimension=1, tiled=True)  41.8 us
    mul x1, other arithmetic, body(): response = -4.0 * jnp.sum(orbitals * shifted(solution), axis=0)  23.9 us
    ppermute x5, starting transfers between devices, extended(): before = lax.ppermute(last, axis, up)  20 us
  transfers between devices with their start and end apart: 11, of which 1 were waited for; matrix products, arithmetic and copies ran while one was open for 15% of the time, Pallas kernels for 0%

commit v1 on v0

v1 whole, which is shorter than its diff:
```python
import functools

import jax
import jax.numpy as jnp
import numpy as np
from jax import lax
from jax.experimental import pallas as pl
from jax.experimental.pallas import tpu as pltpu
from jax.sharding import PartitionSpec as P

STENCIL = (
    -5369.0 / 1800.0,
    12.0 / 7.0,
    -15.0 / 56.0,
    10.0 / 189.0,
    -1.0 / 112.0,
    2.0 / 1925.0,
    -1.0 / 16632.0,
)
SPACING = 0.75
REACH = len(STENCIL) - 1
COEFS = tuple(-0.5 / (SPACING * SPACING) * c for c in STENCIL)
STRIP = 8


def circulant(size):
    full = np.zeros((size, size), np.float64)
    for row in range(size):
        for k in range(1, REACH + 1):
            full[row, (row + k) % size] += COEFS[k]
            full[row, (row - k) % size] += COEFS[k]
    high = full.astype(jnp.bfloat16)
    low = (full - high.astype(np.float64)).astype(jnp.bfloat16)
    return high, low


def kernel(
    n, chunks,
    orb_hbm, pot_hbm, tri_hbm, eig, freq, cz_hbm, cy_hbm,
    sol_hbm, den_hbm,
    orb, pot, tri, src, img, two, res, dirn, fin, cz, cy,
    hup, hlo, sums, coef, part, got, last,
    ld_sem, mat_sem, out_sem,
    dn_s, dn_r, up_s, up_r, sum_s, sum_r, part_s, part_r, last_s, last_r,
):
    planes, ny, nz = src.shape
    wide = coef.shape[1]
    quarter = part.shape[2]
    g = lax.axis_index("grid")
    o = lax.axis_index("orb")
    below, above = lax.rem(g + n - 1, n), lax.rem(g + 1, n)
    has_low, has_up = g > 0, g < n - 1
    odd = lax.rem(g, 2)
    flip1 = o + 1 - 2 * lax.rem(o, 2)
    flip2 = lax.rem(o + 2, 4)
    first = (1 - odd) * flip1 + odd * flip2
    second = odd * flip1 + (1 - odd) * flip2
    both = 3 - o
    energy = eig[0]
    squared = freq[0] * freq[0]

    barrier = pltpu.get_barrier_semaphore()
    for j in range(1, n):
        pl.semaphore_signal(barrier, inc=1, device_id={"grid": lax.rem(g + j, n)})
    pl.semaphore_signal(barrier, inc=1, device_id={"orb": first})
    pl.semaphore_signal(barrier, inc=1, device_id={"orb": second})

    order = []
    for k in range(REACH):
        order += [k, planes - 1 - k]
    order += list(range(REACH, planes - REACH))

    def load(which, p):
        hbm, ref = ((orb_hbm, orb), (tri_hbm, tri))[which]
        return pltpu.make_async_copy(hbm.at[p], ref.at[p], ld_sem.at[which, p])

    for p in order:
        load(0, p).start()
        load(1, p).start()
    mats = [
        pltpu.make_async_copy(cz_hbm, cz, mat_sem.at[0]),
        pltpu.make_async_copy(cy_hbm, cy, mat_sem.at[1]),
        pltpu.make_async_copy(pot_hbm, pot, mat_sem.at[2]),
    ]
    for copy in mats:
        copy.start()

    fields = (src, img, res)

    def down(r, k):
        return pltpu.make_async_remote_copy(
            src_ref=fields[r].at[k], dst_ref=hup.at[r, k],
            send_sem=dn_s.at[r, k], recv_sem=dn_r.at[r, k],
            device_id={"grid": below}, device_id_type=pl.DeviceIdType.MESH)

    def up(r, k):
        return pltpu.make_async_remote_copy(
            src_ref=fields[r].at[planes - 1 - k], dst_ref=hlo.at[r, k],
            send_sem=up_s.at[r, k], recv_sem=up_r.at[r, k],
            device_id={"grid": above}, device_id_type=pl.DeviceIdType.MESH)

    def send(r, p):
        if p < REACH:
            @pl.when(has_low)
            def _():
                down(r, p).start()
        if p >= planes - REACH:
            @pl.when(has_up)
            def _():
                up(r, planes - 1 - p).start()

    def rows_of(s, count):
        return pl.ds(pl.multiple_of(s * count, count), count)

    def over(step, init, count=wide):
        return lax.fori_loop(0, ny // count, step, init)

    zero = jnp.zeros((wide, nz), jnp.float32)

    def upper_pairs(k):
        return [(p, COEFS[planes + k - p]) for p in range(planes - REACH + k, planes)]

    def lower_pairs(k):
        return [(p, COEFS[p + 1 + k]) for p in range(0, REACH - k)]

    def add_halo(acc, halo, pairs):
        def step(s, carry):
            rows = rows_of(s, wide)
            value = halo[rows, :]
            for p, c in pairs:
                acc[p, rows, :] = acc[p, rows, :] + c * value
            return carry

        over(step, 0)

    def arrive(r, k, acc, upper=None, lower=None):
        @pl.when(has_up)
        def _():
            down(r, k).wait_recv()
            add_halo(acc, hup.at[r, k], upper_pairs(k))

        @pl.when(has_low)
        def _():
            up(r, k).wait_recv()
            add_halo(acc, hlo.at[r, k], lower_pairs(k))

    def square_of(ref, p, total):
        def step(s, carry):
            value = ref[p, rows_of(s, wide), :]
            return carry + value * value

        return over(step, total)

    def interior(value, out):
        def plane(p, carry):
            whole = value[p]
            high = whole.astype(jnp.bfloat16)
            low = (whole - high.astype(jnp.float32)).astype(jnp.bfloat16)
            along_z = jnp.dot(
                jnp.concatenate([high, low, high], axis=1), cz[...],
                preferred_element_type=jnp.float32)
            along_y = jnp.dot(
                cy[...], jnp.concatenate([high, low, high], axis=0),
                preferred_element_type=jnp.float32)
            out[p] = along_z + along_y
            return carry

        lax.fori_loop(0, planes, plane, 0)

        def strip(s, carry):
            rows = rows_of(s, STRIP)
            parts = [value[q, rows, :] for q in range(planes)]
            for p in range(planes):
                total = out[p, rows, :] + (pot[p, rows, :] + (3.0 * COEFS[0] - energy)) * parts[p]
                for k in range(1, REACH + 1):
                    near = [parts[q] for q in (p - k, p + k) if 0 <= q < planes]
                    if near:
                        total = total + COEFS[k] * (near[0] + near[1] if len(near) == 2 else near[0])
                out[p, rows, :] = total
            return carry

        over(strip, 0, STRIP)

    def fold(total):
        total = functools.reduce(
            lambda a, b: a + b, [total[i:i + 8] for i in range(0, wide, 8)])
        return functools.reduce(
            lambda a, b: a + b, [total[:, i:i + 128] for i in range(0, nz, 128)])

    def exchange(r, j, slot):
        return pltpu.make_async_remote_copy(
            src_ref=sums.at[r, slot], dst_ref=sums.at[r, slot],
            send_sem=sum_s.at[r, j], recv_sem=sum_r.at[r, j],
            device_id={"grid": lax.rem(g + j, n)}, device_id_type=pl.DeviceIdType.MESH)

    def post(r, *totals):
        for i, total in enumerate(totals):
            sums[r, g, i] = fold(total)
        for i in range(len(totals), sums.shape[2]):
            sums[r, g, i] = jnp.zeros(sums.shape[3:], jnp.float32)
        for j in range(1, n):
            exchange(r, j, g).start()

    def collect(r, i):
        total = sums[r, 0, i]
        for m in range(1, n):
            total = total + sums[r, m, i]
        return jnp.sum(total, keepdims=True)

    def await_sums(r):
        for j in range(1, n):
            exchange(r, j, lax.rem(g + n - j, n)).wait_recv()

    def keep(i, value):
        coef[i] = jnp.broadcast_to(value, (wide, nz))

    pl.semaphore_wait(barrier, n + 1)
    total_src = zero
    for p in order:
        load(0, p).wait()
        load(1, p).wait()

        def step(s, carry, p=p):
            rows = rows_of(s, wide)
            value = orb[p, rows, :] * tri[p, rows, :]
            src[p, rows, :] = value
            return carry + value * value

        total_src = over(step, total_src)
        send(0, p)
    for copy in mats:
        copy.wait()

    interior(src, img)
    total_img = zero
    for p in range(REACH, planes - REACH):
        total_img = square_of(img, p, total_img)
    for k in range(REACH):
        arrive(0, k, img)
        for p in (REACH - 1 - k, planes - REACH + k):
            total_img = square_of(img, p, total_img)
            send(1, p)
    post(0, total_src, total_img)

    interior(img, two)
    for k in range(REACH - 1, 0, -1):
        arrive(1, k, two)
    await_sums(0)
    norm0 = collect(0, 0)
    step0 = norm0 / (collect(0, 1) + squared * norm0)
    keep(0, step0)
    arrive(1, 0, two)
    total_res = zero
    for p in order:
        def step(s, carry, p=p):
            rows = rows_of(s, wide)
            start = src[p, rows, :]
            value = start - coef[0] * (two[p, rows, :] + squared * start)
            res[p, rows, :] = value
            return carry + value * value

        total_res = over(step, total_res)
        send(2, p)
    post(1, total_res)

    interior(res, fin)
    await_sums(1)
    norm1 = collect(1, 0)
    keep(1, norm1 / norm0)

    def direct(p, total):
        def step(s, carry):
            rows = rows_of(s, wide)
            value = res[p, rows, :] + coef[1] * src[p, rows, :]
            dirn[p, rows, :] = value
            fin[p, rows, :] = fin[p, rows, :] + coef[1] * img[p, rows, :]
            return carry + value * value

        return over(step, total)

    total_dir = lax.fori_loop(0, planes, direct, zero)
    total_fin = zero
    for p in range(REACH, planes - REACH):
        total_fin = square_of(fin, p, total_fin)
    for k in range(REACH):
        arrive(2, k, fin)
        for p in (REACH - 1 - k, planes - REACH + k):
            total_fin = square_of(fin, p, total_fin)
    post(2, total_dir, total_fin)
    await_sums(2)
    keep(2, norm1 / (collect(2, 1) + squared * collect(2, 0)))

    span = planes // chunks
    quarters = (both, first, second, o)

    def respond(slot, c):
        base = quarters[slot] * quarter

        def plane(i, carry):
            p = c * span + i
            rows = pl.ds(pl.multiple_of(base, 8), quarter)
            part[slot, p] = (-4.0 * orb[p, rows, :]) * (
                coef[0, 0:1, :] * img[p, rows, :] + coef[2, 0:1, :] * fin[p, rows, :])
            return carry

        lax.fori_loop(0, span, plane, 0)

    def hand(slot, c):
        some = pl.ds(c * span, span)
        return pltpu.make_async_remote_copy(
            src_ref=part.at[slot, some], dst_ref=got.at[slot, some],
            send_sem=part_s.at[slot, c], recv_sem=part_r.at[slot, c],
            device_id={"orb": first}, device_id_type=pl.DeviceIdType.MESH)

    def hand_last(c):
        some = pl.ds(c * span, span)
        return pltpu.make_async_remote_copy(
            src_ref=part.at[2, some], dst_ref=last.at[some],
            send_sem=last_s.at[c], recv_sem=last_r.at[c],
            device_id={"orb": second}, device_id_type=pl.DeviceIdType.MESH)

    for slot in (0, 1):
        for c in range(chunks):
            respond(slot, c)
            hand(slot, c).start()
    for slot in (2, 3):
        for c in range(chunks):
            respond(slot, c)

    for k in range(REACH):
        @pl.when(has_low)
        def _():
            down(0, k).wait_send()

        @pl.when(has_up)
        def _():
            up(0, k).wait_send()

    def solve(p, carry):
        def step(s, inner):
            rows = rows_of(s, wide)
            src[p, rows, :] = coef[0] * src[p, rows, :] + coef[2] * dirn[p, rows, :]
            return inner

        return over(step, carry)

    lax.fori_loop(0, planes, solve, 0)
    out_sol = pltpu.make_async_copy(src, sol_hbm, out_sem.at[0])
    out_sol.start()

    for c in range(chunks):
        hand(0, c).wait_recv()
        some = slice(c * span, (c + 1) * span)
        part[2, some] = part[2, some] + got[0, some]
        hand_last(c).start()
    for c in range(chunks):
        hand(1, c).wait_recv()
        hand_last(c).wait_recv()
        some = slice(c * span, (c + 1) * span)
        part[3, some] = part[3, some] + (got[1, some] + last[some])
    out_den = pltpu.make_async_copy(part.at[3], den_hbm, out_sem.at[1])
    out_den.start()

    for r in (1, 2):
        for k in range(REACH):
            @pl.when(has_low)
            def _():
                down(r, k).wait_send()

            @pl.when(has_up)
            def _():
                up(r, k).wait_send()
    for r in range(3):
        for j in range(1, n):
            exchange(r, j, g).wait_send()
    for c in range(chunks):
        hand(0, c).wait_send()
        hand(1, c).wait_send()
        hand_last(c).wait_send()
    out_sol.wait()
    out_den.wait()


def body(n, groups, orbitals, potential, trial_potential, eigenvalues, frequency):
    count, planes, ny, nz = orbitals.shape
    assert count == 1 and groups == 4 and planes >= 2 * REACH
    quarter = ny // groups
    wide = 32 if ny % 32 == 0 else 8
    chunks = 4 if planes % 4 == 0 else 1
    zh, zl = circulant(nz)
    yh, yl = circulant(ny)
    cz = jnp.asarray(np.concatenate([zh, zh, zl], axis=0))
    cy = jnp.asarray(np.concatenate([yh, yh, yl], axis=1))
    f32 = jnp.float32
    field = pltpu.VMEM((planes, ny, nz), f32)
    dma = pltpu.SemaphoreType.DMA
    anywhere = pl.BlockSpec(memory_space=pl.ANY)
    smem = pl.BlockSpec(memory_space=pltpu.SMEM)
    sol, den = pl.pallas_call(
        functools.partial(kernel, n, chunks),
        out_shape=(
            jax.ShapeDtypeStruct((planes, ny, nz), f32),
            jax.ShapeDtypeStruct((planes, quarter, nz), f32),
        ),
        in_specs=[anywhere] * 3 + [smem] * 2 + [anywhere] * 2,
        out_specs=(anywhere, anywhere),
        scratch_shapes=[field] * 9 + [
            pltpu.VMEM(cz.shape, cz.dtype),
            pltpu.VMEM(cy.shape, cy.dtype),
            pltpu.VMEM((3, REACH, ny, nz), f32),
            pltpu.VMEM((3, REACH, ny, nz), f32),
            pltpu.VMEM((3, n, 2, 8, 128), f32),
            pltpu.VMEM((3, wide, nz), f32),
            pltpu.VMEM((4, planes, quarter, nz), f32),
            pltpu.VMEM((2, planes, quarter, nz), f32),
            pltpu.VMEM((planes, quarter, nz), f32),
            dma((2, planes)), dma((3,)), dma((2,)),
            dma((3, REACH)), dma((3, REACH)), dma((3, REACH)), dma((3, REACH)),
            dma((3, n)), dma((3, n)),
            dma((2, chunks)), dma((2, chunks)), dma((chunks,)), dma((chunks,)),
        ],
        compiler_params=pltpu.CompilerParams(
            collective_id=0, has_side_effects=True, vmem_limit_bytes=60 * 2**20),
        name="sternheimer",
    )(
        orbitals.reshape(planes, ny, nz), potential, trial_potential,
        eigenvalues, frequency, cz, cy,
    )
    return sol.reshape(orbitals.shape), den


def solution(mesh):
    in_specs = (
        P("orb", "grid", None, None),
        P("grid", None, None),
        P("grid", None, None),
        P("orb"),
        P(),
    )
    out_specs = (P("orb", "grid", None, None), P("grid", "orb", None))
    call = functools.partial(body, mesh.shape["grid"], mesh.shape["orb"])
    return jax.shard_map(call, mesh=mesh, in_specs=in_specs, out_specs=out_specs, check_vma=False)
```

time: 445 us -> 88.5 us (0.20); the launches traced: 439 us -> 88.3 us
  other arithmetic: 159 us -> 0 us
  local copies, waits for them, and re-layouts: 144 us -> 4.1 us
  Pallas kernels: 0 us -> 82.3 us
  blocking collectives: 45.9 us -> 0 us
  waiting for transfers between devices: 41.8 us -> 0 us
  starting transfers between devices: 26.5 us -> 0 us
  between operations: 21.8 us -> 1.94 us
    slice x65 -> x0, local copies, waits for them, and re-layouts: 144 us -> none  [the longest x36 86.2 us: shifted_hamiltonian(): jnp.roll(center, -offset, -1)]
    pallas_call x0 -> x1, Pallas kernels: none -> 82.3 us  [body(): pl.pallas_call(functools.partial(kernel, n, chunks), out_shape=(jax.Shape...]
    reduce_sum x3 -> x0, other arithmetic: 59.6 us -> none  [cell_sum(): return jnp.sum(first * second, axis=(1, 2, 3))]
    add x3 -> x0, other arithmetic: 53.7 us -> none  [the longest x2 51.7 us: shifted_hamiltonian(): return -0.5 / (SPACING * SPACING) * summed + (potential - energy) * center]
    psum x2 -> x0, blocking collectives: 45.9 us -> none  [paired(): return lax.psum((cell_sum(vector, vector), cell_sum(vector, image)), 'grid')]
    reduce_scatter x1 -> x0, waiting for transfers between devices: 41.8 us -> none  [body(): density = lax.psum_scatter(response, 'orb', scatter_dimension=1, tiled=True)]
    mul x2 -> x0, other arithmetic: 26.6 us -> none  [the longest x1 23.9 us: body(): response = -4.0 * jnp.sum(orbitals * shifted(solution), axis=0)]
    ppermute x10 -> x0, starting transfers between devices: 26.4 us -> none  [the longest x5 20 us: extended(): before = lax.ppermute(last, axis, up)]
  transfers between devices with their start and end apart: 11 -> 0, of which waited for: 1 -> 0; matrix products, arithmetic and copies ran while one was open for 15% -> 0% of each run, Pallas kernels for 0% -> 0%
where the time goes in v1:
time: 88.5 us; the launch traced here: 88.3 us
  Pallas kernels  82.3 us (93%)
  local copies, waits for them, and re-layouts  4.1 us (5%)
  between operations  1.94 us (2%)
    pallas_call x1, Pallas kernels, body(): pl.pallas_call(functools.partial(kernel, n, chunks), out_shape=(jax.Shape...  82.3 us
    unnamed x4, local copies, waits for them, and re-layouts  4.1 us

profile of v1, /device:TPU:0, one launch (start us, length us, event | category | flops | bytes accessed | tf_op | source)
XLA Modules:
  0.0 88.3 jit_solution(1030424323736551289)
XLA Ops:
  1.9 82.3 %sternheimer.1 = (f32[12,192,256]{2,1,0:T(8,128)}, f32[12,48,256]{2,1,0:T(8,128)}) custom-call(f32[12,192,256]{2,1,0:T(8,128)} %bitcast.3, f32[12,192,256]{2,1,0:T(8,128)} %pot_hbm.1, f32[12,192,256]{2,1,0:T(8,128)} %tri_hbm.1, f32[1]{0:T(128)S(6)} %copy.11.eig, f32[1]{0:T(128)S(6)} %copy.12.freq, bf16[768,256]{1,0:T(8,128)(2,1)} %constant.4.clone.cz_hbm, ...), custom_call_target="tpu_custom_call" | custom-call | tf_op jit(solution)/shard_map/sternheimer/pallas_call | solution.py:399
  84.2 0.0 copy-start
  84.2 3.3 %copy.13 = f32[1,12,192,256]{3,2,1,0:T(8,128)} copy(f32[1,12,192,256]{3,2,1,0:T(8,128)} %bitcast.2) | data formatting | bytes 4718592
  87.5 0.0 copy-done
  87.5 0.8 copy.14
Async XLA Ops:
  84.2 3.3 %copy-start = (f32[12,48,256]{2,1,0:T(8,128)S(1)}, f32[12,48,256]{2,1,0:T(8,128)}, u32[]{:S(2)}) copy-start(f32[12,48,256]{2,1,0:T(8,128)} %get-tuple-element.9) | copy-start | bytes 1769476

commit v2 on v1

--- a/solution.py
+++ b/solution.py
@@ -35,13 +35,14 @@
 
 
 def kernel(
-    n, chunks,
+    n,
     orb_hbm, pot_hbm, tri_hbm, eig, freq, cz_hbm, cy_hbm,
     sol_hbm, den_hbm,
     orb, pot, tri, src, img, two, res, dirn, fin, cz, cy,
-    hup, hlo, sums, coef, part, got, last,
+    hup, hlo, sums, coef, part, got, last, ship, land, mix, dens,
     ld_sem, mat_sem, out_sem,
     dn_s, dn_r, up_s, up_r, sum_s, sum_r, part_s, part_r, last_s, last_r,
+    ship_s, ship_r, mix_s, mix_r,
 ):
     planes, ny, nz = src.shape
     wide = coef.shape[1]
@@ -64,6 +65,7 @@
         pl.semaphore_signal(barrier, inc=1, device_id={"grid": lax.rem(g + j, n)})
     pl.semaphore_signal(barrier, inc=1, device_id={"orb": first})
     pl.semaphore_signal(barrier, inc=1, device_id={"orb": second})
+    pl.semaphore_signal(barrier, inc=1, device_id={"orb": both})
 
     order = []
     for k in range(REACH):
@@ -108,6 +110,27 @@
             @pl.when(has_up)
             def _():
                 up(r, planes - 1 - p).start()
+
+    edge = planes // 4
+    middle = range(edge, planes - edge)
+    outer = list(range(edge)) + list(range(planes - edge, planes))
+    quarters = (both, first, second, o)
+
+    def rows_in(slot):
+        return pl.ds(pl.multiple_of(quarters[slot] * quarter, 8), quarter)
+
+    def ship_copy(field, slot, p):
+        return pltpu.make_async_remote_copy(
+            src_ref=ship.at[field, slot, p - edge], dst_ref=land.at[field, slot, p - edge],
+            send_sem=ship_s.at[field, slot, p - edge], recv_sem=ship_r.at[field, slot, p - edge],
+            device_id={"orb": quarters[slot]}, device_id_type=pl.DeviceIdType.MESH)
+
+    def share(field, value, p):
+        if p in middle:
+            for slot in range(3):
+                rows = rows_in(slot)
+                ship[field, slot, p - edge] = orb[p, rows, :] * value[p, rows, :]
+                ship_copy(field, slot, p).start()
 
     def rows_of(s, count):
         return pl.ds(pl.multiple_of(s * count, count), count)
@@ -196,8 +219,8 @@
     def post(r, *totals):
         for i, total in enumerate(totals):
             sums[r, g, i] = fold(total)
-        for i in range(len(totals), sums.shape[2]):
-            sums[r, g, i] = jnp.zeros(sums.shape[3:], jnp.float32)
+        if len(totals) == 1:
+            sums[r, g, 1] = jnp.zeros(sums.shape[3:], jnp.float32)
         for j in range(1, n):
             exchange(r, j, g).start()
 
@@ -214,7 +237,7 @@
     def keep(i, value):
         coef[i] = jnp.broadcast_to(value, (wide, nz))
 
-    pl.semaphore_wait(barrier, n + 1)
+    pl.semaphore_wait(barrier, n + 2)
     total_src = zero
     for p in order:
         load(0, p).wait()
@@ -235,12 +258,20 @@
     total_img = zero
     for p in range(REACH, planes - REACH):
         total_img = square_of(img, p, total_img)
+    held = []
     for k in range(REACH):
         arrive(0, k, img)
         for p in (REACH - 1 - k, planes - REACH + k):
             total_img = square_of(img, p, total_img)
-            send(1, p)
+            if k < REACH // 2:
+                send(1, p)
+            else:
+                held.append(p)
     post(0, total_src, total_img)
+    for p in held:
+        send(1, p)
+    for p in middle:
+        share(0, img, p)
 
     interior(img, two)
     for k in range(REACH - 1, 0, -1):
@@ -260,72 +291,91 @@
             return carry + value * value
 
         total_res = over(step, total_res)
+        if p in order[:4]:
+            send(2, p)
+    post(1, total_res)
+    for p in order[4:]:
         send(2, p)
-    post(1, total_res)
 
     interior(res, fin)
-    await_sums(1)
-    norm1 = collect(1, 0)
-    keep(1, norm1 / norm0)
 
     def direct(p, total):
         def step(s, carry):
             rows = rows_of(s, wide)
             value = res[p, rows, :] + coef[1] * src[p, rows, :]
             dirn[p, rows, :] = value
-            fin[p, rows, :] = fin[p, rows, :] + coef[1] * img[p, rows, :]
             return carry + value * value
 
         return over(step, total)
 
-    total_dir = lax.fori_loop(0, planes, direct, zero)
+    def square_fin(p, total):
+        def step(s, carry):
+            rows = rows_of(s, wide)
+            value = fin[p, rows, :] + coef[1] * img[p, rows, :]
+            return carry + value * value
+
+        return over(step, total)
+
     total_fin = zero
-    for p in range(REACH, planes - REACH):
-        total_fin = square_of(fin, p, total_fin)
+    done = list(range(REACH, planes - REACH))
+    for p in done:
+        share(1, fin, p)
     for k in range(REACH):
+        if k == REACH - 2:
+            await_sums(1)
+            norm1 = collect(1, 0)
+            ratio = norm1 / norm0
+            keep(1, ratio)
+            total_dir = lax.fori_loop(0, planes, direct, zero)
+            for p in done:
+                total_fin = square_fin(p, total_fin)
         arrive(2, k, fin)
         for p in (REACH - 1 - k, planes - REACH + k):
-            total_fin = square_of(fin, p, total_fin)
+            done.append(p)
+            share(1, fin, p)
+            if k >= REACH - 2:
+                total_fin = square_fin(p, total_fin)
     post(2, total_dir, total_fin)
     await_sums(2)
-    keep(2, norm1 / (collect(2, 1) + squared * collect(2, 0)))
-
-    span = planes // chunks
-    quarters = (both, first, second, o)
-
-    def respond(slot, c):
-        base = quarters[slot] * quarter
-
-        def plane(i, carry):
-            p = c * span + i
-            rows = pl.ds(pl.multiple_of(base, 8), quarter)
-            part[slot, p] = (-4.0 * orb[p, rows, :]) * (
-                coef[0, 0:1, :] * img[p, rows, :] + coef[2, 0:1, :] * fin[p, rows, :])
-            return carry
-
-        lax.fori_loop(0, span, plane, 0)
+    step1 = norm1 / (collect(2, 1) + squared * collect(2, 0))
+    keep(2, step1)
+
+    mix[3, 0] = jnp.broadcast_to(-4.0 * (step0 + step1 * ratio), mix.shape[2:])
+    mix[3, 1] = jnp.broadcast_to(-4.0 * step1, mix.shape[2:])
+
+    def tell(slot):
+        return pltpu.make_async_remote_copy(
+            src_ref=mix.at[3], dst_ref=mix.at[slot],
+            send_sem=mix_s.at[slot], recv_sem=mix_r.at[slot],
+            device_id={"orb": quarters[slot]}, device_id_type=pl.DeviceIdType.MESH)
+
+    for slot in range(3):
+        tell(slot).start()
+
+    def respond(slot, p):
+        rows = rows_in(slot)
+        return orb[p, rows, :] * (
+            mix[3, 0, 0:1, :] * img[p, rows, :] + mix[3, 1, 0:1, :] * fin[p, rows, :])
 
     def hand(slot, c):
-        some = pl.ds(c * span, span)
-        return pltpu.make_async_remote_copy(
-            src_ref=part.at[slot, some], dst_ref=got.at[slot, some],
+        return pltpu.make_async_remote_copy(
+            src_ref=part.at[slot, c], dst_ref=got.at[slot, c],
             send_sem=part_s.at[slot, c], recv_sem=part_r.at[slot, c],
             device_id={"orb": first}, device_id_type=pl.DeviceIdType.MESH)
 
     def hand_last(c):
-        some = pl.ds(c * span, span)
-        return pltpu.make_async_remote_copy(
-            src_ref=part.at[2, some], dst_ref=last.at[some],
+        return pltpu.make_async_remote_copy(
+            src_ref=part.at[2, c], dst_ref=last.at[c],
             send_sem=last_s.at[c], recv_sem=last_r.at[c],
             device_id={"orb": second}, device_id_type=pl.DeviceIdType.MESH)
 
     for slot in (0, 1):
-        for c in range(chunks):
-            respond(slot, c)
+        for c, p in enumerate(outer):
+            part[slot, c] = respond(slot, p)
             hand(slot, c).start()
-    for slot in (2, 3):
-        for c in range(chunks):
-            respond(slot, c)
+    for c, p in enumerate(outer):
+        part[2, c] = respond(2, p)
+        dens[p] = respond(3, p)
 
     for k in range(REACH):
         @pl.when(has_low)
@@ -348,17 +398,24 @@
     out_sol = pltpu.make_async_copy(src, sol_hbm, out_sem.at[0])
     out_sol.start()
 
-    for c in range(chunks):
+    for c in range(len(outer)):
         hand(0, c).wait_recv()
-        some = slice(c * span, (c + 1) * span)
-        part[2, some] = part[2, some] + got[0, some]
+        part[2, c] = part[2, c] + got[0, c]
         hand_last(c).start()
-    for c in range(chunks):
+    for slot in range(3):
+        tell(slot).wait_recv()
+    for p in middle:
+        total = respond(3, p)
+        for slot in range(3):
+            for field in range(2):
+                ship_copy(field, slot, p).wait_recv()
+                total = total + mix[slot, field, 0:1, :] * land[field, slot, p - edge]
+        dens[p] = total
+    for c, p in enumerate(outer):
         hand(1, c).wait_recv()
         hand_last(c).wait_recv()
-        some = slice(c * span, (c + 1) * span)
-        part[3, some] = part[3, some] + (got[1, some] + last[some])
-    out_den = pltpu.make_async_copy(part.at[3], den_hbm, out_sem.at[1])
+        dens[p] = dens[p] + (got[1, c] + last[c])
+    out_den = pltpu.make_async_copy(dens, den_hbm, out_sem.at[1])
     out_den.start()
 
     for r in (1, 2):
@@ -373,7 +430,12 @@
     for r in range(3):
         for j in range(1, n):
             exchange(r, j, g).wait_send()
-    for c in range(chunks):
+    for slot in range(3):
+        tell(slot).wait_send()
+        for p in middle:
+            ship_copy(0, slot, p).wait_send()
+            ship_copy(1, slot, p).wait_send()
+    for c in range(len(outer)):
         hand(0, c).wait_send()
         hand(1, c).wait_send()
         hand_last(c).wait_send()
@@ -386,7 +448,8 @@
     assert count == 1 and groups == 4 and planes >= 2 * REACH
     quarter = ny // groups
     wide = 32 if ny % 32 == 0 else 8
-    chunks = 4 if planes % 4 == 0 else 1
+    edge = planes // 4
+    inner = planes - 2 * edge
     zh, zl = circulant(nz)
     yh, yl = circulant(ny)
     cz = jnp.asarray(np.concatenate([zh, zh, zl], axis=0))
@@ -397,7 +460,7 @@
     anywhere = pl.BlockSpec(memory_space=pl.ANY)
     smem = pl.BlockSpec(memory_space=pltpu.SMEM)
     sol, den = pl.pallas_call(
-        functools.partial(kernel, n, chunks),
+        functools.partial(kernel, n),
         out_shape=(
             jax.ShapeDtypeStruct((planes, ny, nz), f32),
             jax.ShapeDtypeStruct((planes, quarter, nz), f32),
@@ -411,13 +474,18 @@
             pltpu.VMEM((3, REACH, ny, nz), f32),
             pltpu.VMEM((3, n, 2, 8, 128), f32),
             pltpu.VMEM((3, wide, nz), f32),
-            pltpu.VMEM((4, planes, quarter, nz), f32),
-            pltpu.VMEM((2, planes, quarter, nz), f32),
+            pltpu.VMEM((3, 2 * edge, quarter, nz), f32),
+            pltpu.VMEM((2, 2 * edge, quarter, nz), f32),
+            pltpu.VMEM((2 * edge, quarter, nz), f32),
+            pltpu.VMEM((2, 3, inner, quarter, nz), f32),
+            pltpu.VMEM((2, 3, inner, quarter, nz), f32),
+            pltpu.VMEM((4, 2, 8, nz), f32),
             pltpu.VMEM((planes, quarter, nz), f32),
             dma((2, planes)), dma((3,)), dma((2,)),
             dma((3, REACH)), dma((3, REACH)), dma((3, REACH)), dma((3, REACH)),
             dma((3, n)), dma((3, n)),
-            dma((2, chunks)), dma((2, chunks)), dma((chunks,)), dma((chunks,)),
+            dma((2, 2 * edge)), dma((2, 2 * edge)), dma((2 * edge,)), dma((2 * edge,)),
+            dma((2, 3, inner)), dma((2, 3, inner)), dma((3,)), dma((3,)),
         ],
         compiler_params=pltpu.CompilerParams(
             collective_id=0, has_side_effects=True, vmem_limit_bytes=60 * 2**20),

time: 88.5 us -> 76.5 us (0.86)
  Pallas kernels: 82.3 us -> 70.3 us
    pallas_call x1, Pallas kernels: 82.3 us -> 70.3 us  [body(): pl.pallas_call(functools.partial(kernel, n), out_shape=(jax.ShapeDtypeStr...]
where the time goes in v2:
time: 76.5 us; the launch traced here: 76.3 us
  Pallas kernels  70.3 us (92%)
  local copies, waits for them, and re-layouts  4.1 us (5%)
  between operations  1.94 us (3%)
    pallas_call x1, Pallas kernels, body(): pl.pallas_call(functools.partial(kernel, n), out_shape=(jax.ShapeDtypeStr...  70.3 us
    unnamed x4, local copies, waits for them, and re-layouts  4.1 us

profile of v2, /device:TPU:0, one launch (start us, length us, event | category | flops | bytes accessed | tf_op | source)
XLA Modules:
  0.0 76.3 jit_solution(2931383033907704491)
XLA Ops:
  1.9 70.3 %sternheimer.1 = (f32[12,192,256]{2,1,0:T(8,128)}, f32[12,48,256]{2,1,0:T(8,128)}) custom-call(f32[12,192,256]{2,1,0:T(8,128)} %bitcast.3, f32[12,192,256]{2,1,0:T(8,128)} %pot_hbm.1, f32[12,192,256]{2,1,0:T(8,128)} %tri_hbm.1, f32[1]{0:T(128)S(6)} %copy.11.eig, f32[1]{0:T(128)S(6)} %copy.12.freq, bf16[768,256]{1,0:T(8,128)(2,1)} %constant.4.clone.cz_hbm, ...), custom_call_target="tpu_custom_call" | custom-call | tf_op jit(solution)/shard_map/sternheimer/pallas_call | solution.py:462
  72.2 0.0 copy-start
  72.2 3.3 %copy.13 = f32[1,12,192,256]{3,2,1,0:T(8,128)} copy(f32[1,12,192,256]{3,2,1,0:T(8,128)} %bitcast.2) | data formatting | bytes 4718592
  75.5 0.0 copy-done
  75.5 0.8 %copy.14 = f32[12,48,256]{2,1,0:T(8,128)} copy(f32[12,48,256]{2,1,0:T(8,128)S(1)} %copy-done) | data formatting | bytes 1179648
Async XLA Ops:
  72.2 3.3 %copy-start = (f32[12,48,256]{2,1,0:T(8,128)S(1)}, f32[12,48,256]{2,1,0:T(8,128)}, u32[]{:S(2)}) copy-start(f32[12,48,256]{2,1,0:T(8,128)} %get-tuple-element.9) | copy-start | bytes 1769476

commit v3 on v2

--- a/solution.py
+++ b/solution.py
@@ -2,7 +2,6 @@
 
 import jax
 import jax.numpy as jnp
-import numpy as np
 from jax import lax
 from jax.experimental import pallas as pl
 from jax.experimental.pallas import tpu as pltpu
@@ -23,24 +22,32 @@
 STRIP = 8
 
 
-def circulant(size):
-    full = np.zeros((size, size), np.float64)
-    for row in range(size):
+def circulant(ref, count):
+    size = ref.shape[1]
+
+    def step(s, carry):
+        rows = pl.ds(pl.multiple_of(s * count, count), count)
+        row = s * count + lax.broadcasted_iota(jnp.int32, (count, size), 0)
+        apart = jnp.abs(row - lax.broadcasted_iota(jnp.int32, (count, size), 1))
+        apart = jnp.minimum(apart, size - apart)
+        full = jnp.zeros((count, size), jnp.float32)
         for k in range(1, REACH + 1):
-            full[row, (row + k) % size] += COEFS[k]
-            full[row, (row - k) % size] += COEFS[k]
-    high = full.astype(jnp.bfloat16)
-    low = (full - high.astype(np.float64)).astype(jnp.bfloat16)
-    return high, low
+            full = jnp.where(apart == k, COEFS[k], full)
+        high = full.astype(jnp.bfloat16)
+        ref[0, rows, :] = high
+        ref[1, rows, :] = (full - high.astype(jnp.float32)).astype(jnp.bfloat16)
+        return carry
+
+    lax.fori_loop(0, size // count, step, 0)
 
 
 def kernel(
     n,
-    orb_hbm, pot_hbm, tri_hbm, eig, freq, cz_hbm, cy_hbm,
-    sol_hbm, den_hbm,
-    orb, pot, tri, src, img, two, res, dirn, fin, cz, cy,
-    hup, hlo, sums, coef, part, got, last, ship, land, mix, dens,
-    ld_sem, mat_sem, out_sem,
+    orb_hbm, pot_hbm, tri_hbm, eig_hbm, freq_hbm,
+    src, dens,
+    orb, pot, tri, img, two, res, dirn, fin, cz, cy,
+    hup, hlo, sums, coef, part, got, last, ship, land, mix,
+    eig, freq, wave_up, wave_down, ld_sem, mat_sem,
     dn_s, dn_r, up_s, up_r, sum_s, sum_r, part_s, part_r, last_s, last_r,
     ship_s, ship_r, mix_s, mix_r,
 ):
@@ -57,12 +64,16 @@
     first = (1 - odd) * flip1 + odd * flip2
     second = odd * flip1 + (1 - odd) * flip2
     both = 3 - o
-    energy = eig[0]
-    squared = freq[0] * freq[0]
 
     barrier = pltpu.get_barrier_semaphore()
-    for j in range(1, n):
-        pl.semaphore_signal(barrier, inc=1, device_id={"grid": lax.rem(g + j, n)})
+    @pl.when(has_low)
+    def _():
+        pl.semaphore_signal(barrier, inc=1, device_id={"grid": below})
+
+    @pl.when(has_up)
+    def _():
+        pl.semaphore_signal(barrier, inc=1, device_id={"grid": above})
+
     pl.semaphore_signal(barrier, inc=1, device_id={"orb": first})
     pl.semaphore_signal(barrier, inc=1, device_id={"orb": second})
     pl.semaphore_signal(barrier, inc=1, device_id={"orb": both})
@@ -80,9 +91,9 @@
         load(0, p).start()
         load(1, p).start()
     mats = [
-        pltpu.make_async_copy(cz_hbm, cz, mat_sem.at[0]),
-        pltpu.make_async_copy(cy_hbm, cy, mat_sem.at[1]),
-        pltpu.make_async_copy(pot_hbm, pot, mat_sem.at[2]),
+        pltpu.make_async_copy(pot_hbm, pot, mat_sem.at[0]),
+        pltpu.make_async_copy(eig_hbm, eig, mat_sem.at[1]),
+        pltpu.make_async_copy(freq_hbm, freq, mat_sem.at[2]),
     ]
     for copy in mats:
         copy.start()
@@ -179,12 +190,9 @@
             whole = value[p]
             high = whole.astype(jnp.bfloat16)
             low = (whole - high.astype(jnp.float32)).astype(jnp.bfloat16)
-            along_z = jnp.dot(
-                jnp.concatenate([high, low, high], axis=1), cz[...],
-                preferred_element_type=jnp.float32)
-            along_y = jnp.dot(
-                cy[...], jnp.concatenate([high, low, high], axis=0),
-                preferred_element_type=jnp.float32)
+            product = functools.partial(jnp.dot, preferred_element_type=jnp.float32)
+            along_z = product(high, cz[0]) + product(low, cz[0]) + product(high, cz[1])
+            along_y = product(cy[0], high) + product(cy[0], low) + product(cy[1], high)
             out[p] = along_z + along_y
             return carry
 
@@ -237,7 +245,7 @@
     def keep(i, value):
         coef[i] = jnp.broadcast_to(value, (wide, nz))
 
-    pl.semaphore_wait(barrier, n + 2)
+    pl.semaphore_wait(barrier, 3 + jnp.minimum(g, 1) + jnp.minimum(n - 1 - g, 1))
     total_src = zero
     for p in order:
         load(0, p).wait()
@@ -253,8 +261,24 @@
         send(0, p)
     for copy in mats:
         copy.wait()
+    energy = eig[0]
+    squared = freq[0] * freq[0]
+
+    circulant(cz, 32)
+    circulant(cy, 32)
+    def pass_on(wave, has_from, has_to, to):
+        @pl.when(has_from)
+        def _():
+            pl.semaphore_wait(wave, 1)
+
+        @pl.when(has_to)
+        def _():
+            pl.semaphore_signal(wave, inc=1, device_id={"grid": to})
 
     interior(src, img)
+    pass_on(wave_up, has_low, has_up, above)
+    pass_on(wave_down, has_up, has_low, below)
+
     total_img = zero
     for p in range(REACH, planes - REACH):
         total_img = square_of(img, p, total_img)
@@ -280,9 +304,26 @@
     norm0 = collect(0, 0)
     step0 = norm0 / (collect(0, 1) + squared * norm0)
     keep(0, step0)
-    arrive(1, 0, two)
+    @pl.when(has_up)
+    def _():
+        down(1, 0).wait_recv()
+
+    @pl.when(has_low)
+    def _():
+        up(1, 0).wait_recv()
+
     total_res = zero
     for p in order:
+        if p < REACH:
+            @pl.when(has_low)
+            def _():
+                add_halo(two, hlo.at[1, 0], [(p, COEFS[p + 1])])
+
+        if p >= planes - REACH:
+            @pl.when(has_up)
+            def _():
+                add_halo(two, hup.at[1, 0], [(p, COEFS[planes - p])])
+
         def step(s, carry, p=p):
             rows = rows_of(s, wide)
             start = src[p, rows, :]
@@ -395,8 +436,6 @@
         return over(step, carry)
 
     lax.fori_loop(0, planes, solve, 0)
-    out_sol = pltpu.make_async_copy(src, sol_hbm, out_sem.at[0])
-    out_sol.start()
 
     for c in range(len(outer)):
         hand(0, c).wait_recv()
@@ -415,8 +454,6 @@
         hand(1, c).wait_recv()
         hand_last(c).wait_recv()
         dens[p] = dens[p] + (got[1, c] + last[c])
-    out_den = pltpu.make_async_copy(dens, den_hbm, out_sem.at[1])
-    out_den.start()
 
     for r in (1, 2):
         for k in range(REACH):
@@ -439,37 +476,44 @@
         hand(0, c).wait_send()
         hand(1, c).wait_send()
         hand_last(c).wait_send()
-    out_sol.wait()
-    out_den.wait()
+
+
+def write_out(sol, den, sol_hbm, den_hbm, sem):
+    copies = [
+        pltpu.make_async_copy(sol, sol_hbm, sem.at[0]),
+        pltpu.make_async_copy(den, den_hbm, sem.at[1]),
+    ]
+    for copy in copies:
+        copy.start()
+    for copy in copies:
+        copy.wait()
 
 
 def body(n, groups, orbitals, potential, trial_potential, eigenvalues, frequency):
     count, planes, ny, nz = orbitals.shape
     assert count == 1 and groups == 4 and planes >= 2 * REACH
+    assert ny % 32 == 0 and nz % 128 == 0 and min(ny, nz) > 2 * REACH
     quarter = ny // groups
-    wide = 32 if ny % 32 == 0 else 8
+    wide = 32
     edge = planes // 4
     inner = planes - 2 * edge
-    zh, zl = circulant(nz)
-    yh, yl = circulant(ny)
-    cz = jnp.asarray(np.concatenate([zh, zh, zl], axis=0))
-    cy = jnp.asarray(np.concatenate([yh, yh, yl], axis=1))
     f32 = jnp.float32
     field = pltpu.VMEM((planes, ny, nz), f32)
     dma = pltpu.SemaphoreType.DMA
     anywhere = pl.BlockSpec(memory_space=pl.ANY)
-    smem = pl.BlockSpec(memory_space=pltpu.SMEM)
+    hbm = pl.BlockSpec(memory_space=pltpu.HBM)
+    vmem = pl.BlockSpec(memory_space=pltpu.VMEM)
     sol, den = pl.pallas_call(
         functools.partial(kernel, n),
         out_shape=(
-            jax.ShapeDtypeStruct((planes, ny, nz), f32),
-            jax.ShapeDtypeStruct((planes, quarter, nz), f32),
+            pltpu.VMEM((planes, ny, nz), f32),
+            pltpu.VMEM((planes, quarter, nz), f32),
         ),
-        in_specs=[anywhere] * 3 + [smem] * 2 + [anywhere] * 2,
-        out_specs=(anywhere, anywhere),
-        scratch_shapes=[field] * 9 + [
-            pltpu.VMEM(cz.shape, cz.dtype),
-            pltpu.VMEM(cy.shape, cy.dtype),
+        in_specs=[hbm] * 5,
+        out_specs=(vmem, vmem),
+        scratch_shapes=[field] * 8 + [
+            pltpu.VMEM((2, nz, nz), jnp.bfloat16),
+            pltpu.VMEM((2, ny, ny), jnp.bfloat16),
             pltpu.VMEM((3, REACH, ny, nz), f32),
             pltpu.VMEM((3, REACH, ny, nz), f32),
             pltpu.VMEM((3, n, 2, 8, 128), f32),
@@ -480,20 +524,30 @@
             pltpu.VMEM((2, 3, inner, quarter, nz), f32),
             pltpu.VMEM((2, 3, inner, quarter, nz), f32),
             pltpu.VMEM((4, 2, 8, nz), f32),
-            pltpu.VMEM((planes, quarter, nz), f32),
-            dma((2, planes)), dma((3,)), dma((2,)),
+            pltpu.SMEM((1,), f32), pltpu.SMEM((1,), f32),
+            pltpu.SemaphoreType.REGULAR, pltpu.SemaphoreType.REGULAR,
+            dma((2, planes)), dma((3,)),
             dma((3, REACH)), dma((3, REACH)), dma((3, REACH)), dma((3, REACH)),
             dma((3, n)), dma((3, n)),
             dma((2, 2 * edge)), dma((2, 2 * edge)), dma((2 * edge,)), dma((2 * edge,)),
             dma((2, 3, inner)), dma((2, 3, inner)), dma((3,)), dma((3,)),
         ],
         compiler_params=pltpu.CompilerParams(
-            collective_id=0, has_side_effects=True, vmem_limit_bytes=60 * 2**20),
+            collective_id=0, has_side_effects=True, vmem_limit_bytes=50 * 2**20),
         name="sternheimer",
     )(
         orbitals.reshape(planes, ny, nz), potential, trial_potential,
-        eigenvalues, frequency, cz, cy,
+        eigenvalues, frequency,
     )
+    sol, den = pl.pallas_call(
+        write_out,
+        out_shape=(jax.ShapeDtypeStruct(sol.shape, f32), jax.ShapeDtypeStruct(den.shape, f32)),
+        in_specs=[vmem] * 2,
+        out_specs=(anywhere, anywhere),
+        scratch_shapes=[dma((2,))],
+        compiler_params=pltpu.CompilerParams(vmem_limit_bytes=2**20),
+        name="write_out",
+    )(sol, den)
     return sol.reshape(orbitals.shape), den
 
 

time: 76.5 us -> 72.9 us (0.953)
  local copies, waits for them, and re-layouts: 4.1 us -> 0 us
    unnamed x4 -> x0, local copies, waits for them, and re-layouts: 4.1 us -> none
    pallas_call x1 -> x2, Pallas kernels: 70.3 us -> 70.8 us  [the longest x1 69.2 us: body(): pl.pallas_call(functools.partial(kernel, n), out_shape=(pltpu.VMEM((plane...]
where the time goes in v3:
time: 72.9 us; the launch traced here: 72.8 us
  Pallas kernels  70.8 us (97%)
  between operations  1.93 us (3%)
    pallas_call x1, Pallas kernels, body(): pl.pallas_call(functools.partial(kernel, n), out_shape=(pltpu.VMEM((plane...  69.2 us
    pallas_call x1, Pallas kernels, body(): pl.pallas_call(write_out, out_shape=(jax.ShapeDtypeStruct(sol.shape, f32)...  1.61 us

profile of v3, /device:TPU:0, one launch (start us, length us, event | category | flops | bytes accessed | tf_op | source)
XLA Modules:
  0.0 72.8 jit_solution(11110249091334726069)
XLA Ops:
  1.9 69.2 %sternheimer.1 = (f32[12,192,256]{2,1,0:T(8,128)S(1)}, f32[12,48,256]{2,1,0:T(8,128)S(1)}) custom-call(f32[12,192,256]{2,1,0:T(8,128)} %bitcast.2, f32[12,192,256]{2,1,0:T(8,128)} %pot_hbm.1, f32[12,192,256]{2,1,0:T(8,128)} %tri_hbm.1, f32[1]{0:T(128)S(6)} %copy.7.eig_hbm, f32[1]{0:T(128)S(6)} %copy.8.freq_hbm), custom_call_target="tpu_custom_call" | custom-call | tf_op jit(solution)/shard_map/sternheimer/pallas_call | solution.py:506
  71.1 1.6 %write_out.1 = (f32[12,192,256]{2,1,0:T(8,128)}, f32[12,48,256]{2,1,0:T(8,128)}) custom-call(f32[12,192,256]{2,1,0:T(8,128)S(1)} %get-tuple-element.6.sol, f32[12,48,256]{2,1,0:T(8,128)S(1)} %get-tuple-element.7.den), custom_call_target="tpu_custom_call" | custom-call | tf_op jit(solution)/shard_map/write_out/pallas_call | solution.py:542

commit v4 on v3

--- a/solution.py
+++ b/solution.py
@@ -122,7 +122,7 @@
             def _():
                 up(r, planes - 1 - p).start()
 
-    edge = planes // 4
+    edge = planes // 6
     middle = range(edge, planes - edge)
     outer = list(range(edge)) + list(range(planes - edge, planes))
     quarters = (both, first, second, o)
@@ -495,7 +495,7 @@
     assert ny % 32 == 0 and nz % 128 == 0 and min(ny, nz) > 2 * REACH
     quarter = ny // groups
     wide = 32
-    edge = planes // 4
+    edge = planes // 6
     inner = planes - 2 * edge
     f32 = jnp.float32
     field = pltpu.VMEM((planes, ny, nz), f32)

time: 72.9 us -> 72.1 us (0.989)
  the two profiles are of different devices: /device:TPU:0 before, /device:TPU:9 now
where the time goes in v4:
time: 72.1 us; the launch traced here: 71.9 us
  Pallas kernels  70 us (97%)
  between operations  1.93 us (3%)
    pallas_call x1, Pallas kernels, body(): pl.pallas_call(functools.partial(kernel, n), out_shape=(pltpu.VMEM((plane...  68.4 us
    pallas_call x1, Pallas kernels, body(): pl.pallas_call(write_out, out_shape=(jax.ShapeDtypeStruct(sol.shape, f32)...  1.61 us

profile of v4, /device:TPU:9, one launch (start us, length us, event | category | flops | bytes accessed | tf_op | source)
XLA Modules:
  0.0 71.9 jit_solution(15981215351349502302)
XLA Ops:
  1.9 68.4 %sternheimer.1 = (f32[12,192,256]{2,1,0:T(8,128)S(1)}, f32[12,48,256]{2,1,0:T(8,128)S(1)}) custom-call(f32[12,192,256]{2,1,0:T(8,128)} %bitcast.2, f32[12,192,256]{2,1,0:T(8,128)} %pot_hbm.1, f32[12,192,256]{2,1,0:T(8,128)} %tri_hbm.1, f32[1]{0:T(128)S(6)} %copy.7.eig_hbm, f32[1]{0:T(128)S(6)} %copy.8.freq_hbm), custom_call_target="tpu_custom_call" | custom-call | tf_op jit(solution)/shard_map/sternheimer/pallas_call | solution.py:506
  70.3 1.6 %write_out.1 = (f32[12,192,256]{2,1,0:T(8,128)}, f32[12,48,256]{2,1,0:T(8,128)}) custom-call(f32[12,192,256]{2,1,0:T(8,128)S(1)} %get-tuple-element.6.sol, f32[12,48,256]{2,1,0:T(8,128)S(1)} %get-tuple-element.7.den), custom_call_target="tpu_custom_call" | custom-call | tf_op jit(solution)/shard_map/write_out/pallas_call | solution.py:542
